TPU v7x, 32 devices: a whole 2x2x4 slice. The times are simulated.
32 devices in a mesh: seq: 16 (over z, y, x), head: 2 (over core).
Axes of the slice: x: 2, y: 2, z: 4, core: 2. Of those that a mesh axis runs over, the one named last changes fastest.
Arguments:
- queries: bfloat16 [4096, 4096], P('seq', 'head'), may hold values from -1.796875 to 1.796875
- key_rows: bfloat16 [4096, 4096], P('seq', 'head'), may hold values from -1.796875 to 1.796875
- values: bfloat16 [4096, 4096], P('seq', 'head'), may hold values from -100 to 100
- out_weight: bfloat16 [4096, 4096], P('head', 'seq'), may hold values from -0.125 to 0.125
- out_grad: bfloat16 [4096, 4096], P('seq', 'head'), may hold values from -6 to 6
Outputs:
- mixed: bfloat16 [4096, 4096], P('seq', 'head')
- query_grad: bfloat16 [4096, 4096], P('seq', 'head')
- key_grad: bfloat16 [4096, 4096], P('seq', 'head')
- value_grad: bfloat16 [4096, 4096], P('seq', 'head')
All inputs are finite; a program needn't handle non-finite values.
Results may differ from a plain program's by a relative error of at most 0.014.
Values may be sent and summed in bfloat16 or wider, within the bound.
A program may use at most 128 MiB of HBM per device.

v0:
```python
import jax
import jax.numpy as jnp
from jax import lax
from jax.sharding import PartitionSpec as P

HEAD_DIM = 128


def prefix_2(value, axis, combine, identity):
    length, position = (lax.axis_size(axis), lax.axis_index(axis))
    everything = lax.all_gather(value, axis)
    start = jnp.broadcast_to(jnp.asarray(identity, value.dtype), value.shape)

    def hop(k, before):
        reached = k < position
        new = combine(before, everything[k])
        return jnp.where(reached, new, before)

    return lax.fori_loop(0, length, hop, start)


def prefix_3(value, axis, combine, identity):
    length, position = (lax.axis_size(axis), lax.axis_index(axis))
    everything = lax.all_gather(value.astype(jnp.bfloat16), axis)
    start = jnp.broadcast_to(jnp.asarray(identity, value.dtype), value.shape)

    def hop(k, before):
        at = length - 1 - k
        reached = at > position
        new = combine(before, everything[at].astype(value.dtype))
        return jnp.where(reached, new, before)

    return lax.fori_loop(0, length, hop, start)


def lower_mask(length):
    row_ids = lax.broadcasted_iota(jnp.int32, (length, length), 0)
    col_ids = lax.broadcasted_iota(jnp.int32, (length, length), 1)
    return row_ids >= col_ids


def add_states(earlier, latter):
    return earlier + latter


def contract_cols(left_side, right_side):
    return lax.dot_general(
        left_side, right_side, (((1,), (1,)), ((), ())), preferred_element_type=jnp.float32
    )


def per_device(queries, key_rows, values, out_weight, out_grad):
    length = queries.shape[0]
    heads_here = queries.shape[1] // HEAD_DIM
    query_heads = queries.reshape(length, heads_here, HEAD_DIM)
    key_heads = key_rows.reshape(length, heads_here, HEAD_DIM)
    value_heads = values.reshape(length, heads_here, HEAD_DIM)
    causal = lower_mask(length)[None]
    local_state = jnp.einsum(
        "shd,she->hde", key_heads, value_heads, preferred_element_type=jnp.float32
    )
    prefix = prefix_2(local_state, "seq", add_states, jnp.zeros_like(local_state))
    prefix_low = prefix.astype(jnp.bfloat16)
    scores = jnp.einsum("thd,shd->hts", query_heads, key_heads, preferred_element_type=jnp.float32)
    weights = jnp.where(causal, scores, 0.0).astype(jnp.bfloat16)
    numerator = jnp.einsum("hts,she->the", weights, value_heads, preferred_element_type=jnp.float32)
    numerator = numerator + jnp.einsum(
        "thd,hde->the", query_heads, prefix_low, preferred_element_type=jnp.float32
    )
    spread = jnp.sqrt(jnp.mean(numerator * numerator, axis=-1, keepdims=True) + 1e-06)
    normed = numerator / spread
    attended = normed.astype(jnp.bfloat16).reshape(length, heads_here * HEAD_DIM)
    full_weight = lax.all_gather(out_weight, "seq", axis=1, tiled=True)
    partial_value = jnp.dot(attended, full_weight, preferred_element_type=jnp.float32)
    layer_out = lax.psum_scatter(
        partial_value.astype(jnp.bfloat16), "head", scatter_dimension=1, tiled=True
    )
    out_dir = contract_cols(lax.all_gather(out_grad, "head", axis=1, tiled=True), full_weight)
    out_dir = out_dir.reshape(length, heads_here, HEAD_DIM)
    along_dir = jnp.mean(out_dir * normed, axis=-1, keepdims=True)
    numer_grad = ((out_dir - normed * along_dir) / spread).astype(jnp.bfloat16)
    local_grad = jnp.einsum(
        "thd,the->hde", query_heads, numer_grad, preferred_element_type=jnp.float32
    )
    suffix = prefix_3(local_grad, "seq", add_states, jnp.zeros_like(local_grad))
    suffix_low = suffix.astype(jnp.bfloat16)
    pair_scores = jnp.einsum(
        "the,she->hts", numer_grad, value_heads, preferred_element_type=jnp.float32
    )
    pair_low = jnp.where(causal, pair_scores, 0.0).astype(jnp.bfloat16)
    query_out = jnp.einsum("hts,shd->thd", pair_low, key_heads, preferred_element_type=jnp.float32)
    query_out = query_out + jnp.einsum(
        "the,hde->thd", numer_grad, prefix_low, preferred_element_type=jnp.float32
    )
    key_out = jnp.einsum("hts,thd->shd", pair_low, query_heads, preferred_element_type=jnp.float32)
    key_out = key_out + jnp.einsum(
        "she,hde->shd", value_heads, suffix_low, preferred_element_type=jnp.float32
    )
    value_out = jnp.einsum("hts,the->she", weights, numer_grad, preferred_element_type=jnp.float32)
    value_out = value_out + jnp.einsum(
        "shd,hde->she", key_heads, suffix_low, preferred_element_type=jnp.float32
    )
    flat_shape = (length, heads_here * HEAD_DIM)
    return (
        layer_out,
        query_out.reshape(flat_shape).astype(jnp.bfloat16),
        key_out.reshape(flat_shape).astype(jnp.bfloat16),
        value_out.reshape(flat_shape).astype(jnp.bfloat16),
    )


def solution(mesh):
    placed = (
        P("seq", "head"),
        P("seq", "head"),
        P("seq", "head"),
        P("head", "seq"),
        P("seq", "head"),
    )
    return jax.shard_map(
        per_device,
        mesh=mesh,
        in_specs=placed,
        out_specs=(P("seq", "head"), P("seq", "head"), P("seq", "head"), P("seq", "head")),
        check_vma=False,
    )
```

profile of v0, /device:TPU:0, one launch (start us, length us, event | category | flops | bytes accessed | tf_op | source)
XLA Modules:
  0.0 626.5 jit_solution(6565324269693306513)
XLA Ops:
  7.2 2.6 copy.59
  9.8 1.6 copy.33
  11.5 1.4 fusion.7
  12.9 0.7 all-gather.9.cloned.1.call-update
  13.7 0.7 all-gather.7.cloned.1.call-update
  14.5 1.9 select_convert_fusion.1
  16.4 1.3 copy-done.9
  17.7 2.1 fusion.3
  19.9 186.9 %all-gather.11.cloned.1.call-done = f32[256,128,128]{2,1,0:T(8,128)} async-done(((f32[16,128,128]{2,1,0:T(8,128)}), f32[256,128,128]{2,1,0:T(8,128)}) %all-gather.11.cloned.1.call-update) | async-done | bytes 16777232 | tf_op jit(solution)/shard_map/all_gather | solution.py:11
  206.8 26.3 %while.30 = (s32[]{:T(128)}, f32[16,128,128]{2,1,0:T(8,128)S(1)}, s32[]{:T(128)}, f32[16,16,128,128]{3,2,1,0:T(8,128)}, s32[]{:T(128)}, /*index=5*/s32[]{:T(128)}) while((s32[]{:T(128)}, f32[16,128,128]{2,1,0:T(8,128)S(1)}, s32[]{:T(128)}, f32[16,16,128,128]{3,2,1,0:T(8,128)}, s32[]{:T(128)}, /*index=5*/s32[]{:T(128)}) %tuple.93), condition=%wide.region_1.2_spmd.clone, body=%wide.region_0.1_spmd.clone.sunk | while | flops 786436 | bytes 3145829 | solution.py:19
  206.8 1.6 add_select_fusion.4
  208.4 1.6 add_select_fusion.4
  210.0 1.6 add_select_fusion.4
  211.6 1.7 add_select_fusion.4
  213.3 1.7 add_select_fusion.4
  215.1 1.6 add_select_fusion.4
  216.7 1.6 add_select_fusion.4
  218.3 1.6 add_select_fusion.4
  219.9 1.6 add_select_fusion.4
  221.5 1.6 add_select_fusion.4
  223.1 1.6 add_select_fusion.4
  224.8 1.6 add_select_fusion.4
  226.4 1.6 add_select_fusion.4
  228.0 1.7 add_select_fusion.4
  229.7 1.7 add_select_fusion.4
  231.4 1.7 add_select_fusion.4
  233.1 3.4 multiply_reduce_fusion.1
  236.6 219.0 %all-gather.7.cloned.1.call-done = bf16[2048,4096]{1,0:T(8,128)(2,1)} async-done(((bf16[2048,256]{1,0:T(8,128)(2,1)}), bf16[2048,4096]{1,0:T(8,128)(2,1)}) %all-gather.7.cloned.1.call-update) | async-done | bytes 16777232 | tf_op jit(solution)/shard_map/all_gather | solution.py:73
  455.6 12.5 %multiply_reduce_fusion = (f32[256,16]{0,1:T(8,128)S(1)}, f32[256,2048]{0,1:T(8,128)S(1)}) fusion(f32[256,16,128]{0,2,1:T(8,128)} %get-tuple-element.256, f32[256,16]{0,1:T(8,128)S(1)} %add_sqrt_fusion, bf16[256,4096]{1,0:T(8,128)(2,1)} %all-gather.9.cloned.1.call-done, bf16[2048,4096]{1,0:T(8,128)(2,1)} %all-gather.7.cloned.1.call-done), kind=kOutput, calls=%fused_computation.12 | convolution fusion | flops 4296536064 | bytes 23101440 | tf_op jit(solution)/shard_map/dot_general | solution.py:47
  468.1 1.6 divide_convert_fusion
  469.7 1.0 copy-done.2
  470.7 0.4 fusion.2
  471.1 1.0 copy.44
  472.4 2.4 select_convert_fusion
  474.8 0.8 fusion.31
  475.6 0.6 copy-done.11
  476.2 0.6 copy-done.3
  476.8 1.4 fusion.1
  478.2 2.3 copy.48
  480.6 3.6 fusion.11
  484.2 1.8 fusion.32
  485.9 11.6 %convolution_convert_fusion = bf16[256,4096]{1,0:T(8,128)(2,1)} fusion(bf16[256,2048]{0,1:T(8,128)(2,1)S(1)} %bitcast.112, bf16[2048,4096]{1,0:T(8,128)(2,1)} %all-gather.7.cloned.1.call-done), kind=kOutput, calls=%fused_computation.2 | convolution fusion | flops 4296015872 | bytes 19922944 | tf_op jit(solution)/shard_map/dot_general | solution.py:74
  497.5 85.2 %all-gather.13.cloned.1.call-done = bf16[256,128,128]{2,1,0:T(8,128)(2,1)} async-done(((bf16[16,128,128]{2,1,0:T(8,128)(2,1)}), bf16[256,128,128]{2,1,0:T(8,128)(2,1)}) %all-gather.13.cloned.1.call-update) | async-done | bytes 8388624 | tf_op jit(solution)/shard_map/all_gather | solution.py:24
  582.8 26.5 %while.31 = (s32[]{:T(128)}, f32[16,128,128]{2,1,0:T(8,128)S(1)}, s32[]{:T(128)}, bf16[16,16,128,128]{3,2,1,0:T(8,128)(2,1)}, s32[]{:T(128)}, /*index=5*/s32[]{:T(128)}, s32[]{:T(128)}, s32[]{:T(128)}) while((s32[]{:T(128)}, f32[16,128,128]{2,1,0:T(8,128)S(1)}, s32[]{:T(128)}, bf16[16,16,128,128]{3,2,1,0:T(8,128)(2,1)}, s32[]{:T(128)}, ...), condition=%wide.region_6.7_spmd.clone, body=%wide.region_5.6_spmd.clone.sunk | while | flops 1048584 | bytes 2621603 | solution.py:33
  582.8 1.7 add_select_fusion.5
  584.5 1.6 add_select_fusion.5
  586.2 1.6 add_select_fusion.5
  587.8 1.6 add_select_fusion.5
  589.4 1.7 add_select_fusion.5
  591.1 1.6 add_select_fusion.5
  592.8 1.6 add_select_fusion.5
  594.5 1.6 add_select_fusion.5
  596.1 1.6 add_select_fusion.5
  597.7 1.6 add_select_fusion.5
  599.4 1.6 add_select_fusion.5
  601.0 1.6 add_select_fusion.5
  602.7 1.6 add_select_fusion.5
  604.3 1.6 add_select_fusion.5
  606.0 1.6 add_select_fusion.5
  607.6 1.6 add_select_fusion.5
  609.3 3.0 fusion
  612.3 2.4 copy.49
  614.6 3.1 add_convert_fusion
  617.7 2.3 copy.50
  (39 shorter events, 0.6 us)
Async XLA Ops:
  7.2 7.3 %copy-start = (bf16[256,2048]{1,0:T(8,128)(2,1)S(1)}, bf16[256,2048]{1,0:T(8,128)(2,1)}, u32[]{:S(2)}) copy-start(bf16[256,2048]{1,0:T(8,128)(2,1)} %param.9) | copy-start | bytes 3145732
  7.2 199.6 %all-gather.11.cloned.1.call-start = ((), (), s32[]{:S(2)}) async-start(), calls=%async_computation.4 | async-start | bytes 17825792 | tf_op jit(solution)/shard_map/all_gather | solution.py:11
  7.2 4.2 copy-start.5
  11.5 1.4 copy-start.7
  12.9 223.6 %all-gather.9.cloned.1.call-start = ((), (), s32[]{:S(2)}) async-start(), calls=%async_computation.3 | async-start | bytes 3145728 | tf_op jit(solution)/shard_map/all_gather | solution.py:78
  13.6 441.9 %all-gather.7.cloned.1.call-start = ((), (), s32[]{:S(2)}) async-start(), calls=%async_computation.1 | async-start | bytes 17825792 | tf_op jit(solution)/shard_map/all_gather | solution.py:73
  14.4 568.4 %all-gather.13.cloned.1.call-start = ((), (), s32[]{:S(2)}) async-start(), calls=%async_computation.5 | async-start | bytes 8912896 | tf_op jit(solution)/shard_map/all_gather | solution.py:24
  16.4 1.3 copy-start.9
  455.6 12.5 %copy-start.1 = (f32[256,16,128]{0,2,1:T(8,128)S(1)}, f32[256,16,128]{0,2,1:T(8,128)}, u32[]{:S(2)}) copy-start(f32[256,16,128]{0,2,1:T(8,128)} %get-tuple-element.256) | copy-start | bytes 6291460
  469.7 1.0 copy-start.2
  472.1 147.8 %reduce-scatter.2.cloned.1.call-start = ((), (), s32[]{:S(2)}) async-start(), calls=%async_computation.2 | async-start | bytes 3145728 | tf_op jit(solution)/shard_map/reduce_scatter | solution.py:75
  472.4 2.4 copy-start.8
  474.8 1.4 copy-start.11
  474.8 2.0 copy-start.3
  480.6 3.6 copy-start.4
  480.6 3.6 copy-start.10
  484.2 1.8 copy-start.12
  582.8 26.5 %copy-start.6 = (bf16[256,2048]{1,0:T(8,128)(2,1)S(1)}, bf16[256,2048]{1,0:T(8,128)(2,1)}, u32[]{:S(2)}) copy-start(bf16[256,2048]{1,0:T(8,128)(2,1)} %param.11) | copy-start | bytes 3145732
  612.3 2.4 copy-start.13
Sparse Core Ops, SparseCore 0:
  13.0 193.7 all-gather.10
  208.3 8.7 all-gather.8
  219.8 235.7 all-gather.6
  472.3 110.4 all-gather.12
  585.4 7.7 reduce-scatter.1
where the time goes:
time: 628 us; the launch traced here: 626 us
  waiting for transfers between devices  493 us (79%)
  other arithmetic  53.5 us (9%)
  matrix products  49.6 us (8%)
  local copies, waits for them, and re-layouts  15.6 us (2%)
  between operations  14 us (2%)
    all_gather x1, waiting for transfers between devices, per_device(): full_weight = lax.all_gather(out_weight, 'seq', axis=1, tiled=True)  219 us
    all_gather x1, waiting for transfers between devices, prefix_2(): everything = lax.all_gather(value, axis)  187 us
    all_gather x1, waiting for transfers between devices, prefix_3(): everything = lax.all_gather(value.astype(jnp.bfloat16), axis)  85.2 us
    select_n x32, other arithmetic, hop(): return jnp.where(reached, new, before)  52 us
    unnamed x32, local copies, waits for them, and re-layouts  13 us
  transfers between devices with their start and end apart: 5, of which 3 were waited for; matrix products, arithmetic and copies ran while one was open for 15% of the time, Pallas kernels for 0%

commit v1 on v0

--- a/solution.py
+++ b/solution.py
@@ -1,9 +1,15 @@
+import functools
+
 import jax
 import jax.numpy as jnp
 from jax import lax
+from jax.experimental import pallas as pl
+from jax.experimental.pallas import tpu as pltpu
 from jax.sharding import PartitionSpec as P
 
 HEAD_DIM = 128
+MESH = pl.DeviceIdType.MESH
+PLANE = 4
 
 
 def prefix_2(value, axis, combine, identity):
@@ -47,6 +53,16 @@
     return lax.dot_general(
         left_side, right_side, (((1,), (1,)), ((), ())), preferred_element_type=jnp.float32
     )
+
+
+def contract_rows(left_side, right_side):
+    return lax.dot_general(
+        left_side, right_side, (((0,), (0,)), ((), ())), preferred_element_type=jnp.float32
+    )
+
+
+def contract_mid(left_side, right_side):
+    return jnp.dot(left_side, right_side, preferred_element_type=jnp.float32)
 
 
 def per_device(queries, key_rows, values, out_weight, out_grad):
@@ -109,7 +125,406 @@
     )
 
 
+def visit_tables(planes):
+    rows = []
+    for own in range(planes):
+        near_low = own < planes - 1 - own
+        rows.append(sorted(range(planes), key=lambda other: (abs(other - own), (other > own) == near_low)))
+    return rows
+
+
+def pick(table, position):
+    found = jnp.int32(table[0])
+    for at in range(1, len(table)):
+        found = jnp.where(position == at, jnp.int32(table[at]), found)
+    return found
+
+
+def kernel(
+    blocks, q_ref, k_ref, v_ref, w_ref, g_ref,
+    mixed_ref, dq_ref, dk_ref, dv_ref,
+    w_all, g_all, st_send, st_recv, pre_send, prefix, lg_send, lg_recv, suf_send, suffix,
+    out_dir, normed, inv_spread, weights, attended, p_own, p_send, p_recv, ng, k_part, v_part,
+    w_recv_sem, wx_sem, wy_sem, wz_sem, local_sem, g_sem, a_send_sem, a_recv_sem, p_send_sem, p_recv_sem,
+):
+    me = lax.axis_index("seq")
+    core = lax.axis_index("head")
+    other = 1 - core
+    planes = blocks // PLANE
+    spot = lax.rem(me, PLANE)
+    level = me // PLANE
+    bit_x, bit_y = lax.rem(spot, 2), spot // 2
+    spot_x = spot + 1 - 2 * bit_x
+    spot_y = spot + 2 - 4 * bit_y
+    spot_d = spot_x + 2 - 4 * bit_y
+    length, width = q_ref.shape
+    heads = width // HEAD_DIM
+    rows, cols = w_ref.shape
+    half = rows // 2
+    per_core = blocks // 2
+
+    def at_seq(position):
+        return (position, core)
+
+    nbr_x = level * PLANE + spot_x
+    nbr_y = level * PLANE + spot_y
+
+    barrier = pltpu.get_barrier_semaphore()
+
+    def greet(i, carry):
+        pl.semaphore_signal(barrier, inc=1, device_id=at_seq(lax.rem(me + i, blocks)), device_id_type=MESH)
+        return carry
+
+    lax.fori_loop(1, blocks, greet, 0)
+    pl.semaphore_signal(barrier, inc=1, device_id=(me, other), device_id_type=MESH)
+
+    own_w = pltpu.make_async_copy(w_ref, w_all.at[me], local_sem.at[0])
+    own_g = pltpu.make_async_copy(g_ref, g_all.at[core], local_sem.at[1])
+    own_w.start()
+    own_g.start()
+
+    def head_cols(h):
+        return pl.ds(pl.multiple_of(h * HEAD_DIM, HEAD_DIM), HEAD_DIM)
+
+    def make_state(h, carry):
+        c = head_cols(h)
+        st_send[h] = contract_rows(k_ref[:, c], v_ref[:, c]).astype(jnp.bfloat16)
+        return carry
+
+    lax.fori_loop(0, heads, make_state, 0)
+    st_recv[me] = st_send[me]
+
+    pl.semaphore_wait(barrier, blocks)
+
+    def exchange(src, dst, kind, start):
+        def one(i, carry):
+            peer = lax.rem(me + i, blocks)
+            copy = pltpu.make_async_remote_copy(
+                src_ref=src.at[peer], dst_ref=dst.at[me],
+                send_sem=a_send_sem.at[kind, peer], recv_sem=a_recv_sem.at[kind, me],
+                device_id=at_seq(peer), device_id_type=MESH,
+            )
+            if start:
+                copy.start()
+            else:
+                copy.wait_send()
+            return carry
+
+        lax.fori_loop(1, blocks, one, 0)
+
+    def arrived(src, dst, kind):
+        def one(i, carry):
+            peer = lax.rem(me + i, blocks)
+            pltpu.make_async_remote_copy(
+                src_ref=src.at[me], dst_ref=dst.at[peer],
+                send_sem=a_send_sem.at[kind, me], recv_sem=a_recv_sem.at[kind, peer],
+                device_id=at_seq(peer), device_id_type=MESH,
+            ).wait_recv()
+            return carry
+
+        lax.fori_loop(1, blocks, one, 0)
+
+    g_copy = pltpu.make_async_remote_copy(
+        src_ref=g_ref, dst_ref=g_all.at[core], send_sem=g_sem.at[0], recv_sem=g_sem.at[1],
+        device_id=(me, other), device_id_type=MESH,
+    )
+    g_copy.start()
+    exchange(st_send, st_recv, 0, True)
+
+    def piece(block, part, sems, target, own=False):
+        span = pl.ds(part * half, half)
+        return pltpu.make_async_remote_copy(
+            src_ref=w_ref.at[span] if own else w_all.at[block, span],
+            dst_ref=w_all.at[block, span],
+            send_sem=sems.at[block, part], recv_sem=w_recv_sem.at[block, part],
+            device_id=at_seq(target), device_id_type=MESH,
+        )
+
+    up_ok = level + 1 < planes
+    down_ok = level > 0
+    up = jnp.minimum(me + PLANE, blocks - PLANE + spot)
+    down = jnp.maximum(me - PLANE, spot)
+
+    for part in range(2):
+        piece(me, part, wx_sem, nbr_x, True).start()
+        piece(me, part, wy_sem, nbr_y, True).start()
+
+        @pl.when(up_ok)
+        def _():
+            piece(me, part, wz_sem.at[0], up, True).start()
+
+        @pl.when(down_ok)
+        def _():
+            piece(me, part, wz_sem.at[1], down, True).start()
+
+    tables = visit_tables(planes)
+    order = [pick([tables[z][k] for z in range(planes)], level) for k in range(planes)]
+
+    def column_step(k, finish=False):
+        plane = order[k]
+        block = plane * PLANE + spot
+        going_up = plane < level
+        for part in range(2):
+            if not finish:
+                piece(block, part, wx_sem, nbr_x).wait_recv()
+                piece(block, part, wx_sem, nbr_x).start()
+                piece(block, part, wy_sem, nbr_y).start()
+
+            @pl.when(jnp.logical_and(going_up, up_ok))
+            def _():
+                copy = piece(block, part, wz_sem.at[0], up)
+                copy.wait_send() if finish else copy.start()
+
+            @pl.when(jnp.logical_and(jnp.logical_not(going_up), down_ok))
+            def _():
+                copy = piece(block, part, wz_sem.at[1], down)
+                copy.wait_send() if finish else copy.start()
+
+            if finish:
+                piece(block, part, wx_sem, nbr_x).wait_send()
+                piece(block, part, wy_sem, nbr_y).wait_send()
+
+    def relay_step(k, finish=False):
+        plane = order[k]
+        to_x = piece(plane * PLANE + spot_y, 0, wx_sem, nbr_x)
+        to_y = piece(plane * PLANE + spot_x, 1, wy_sem, nbr_y)
+        for copy in (to_x, to_y):
+            if finish:
+                copy.wait_send()
+            else:
+                copy.wait_recv()
+                copy.start()
+
+    def settle(k):
+        plane = order[k]
+        for where, part in ((spot_y, 1), (spot_x, 0), (spot_d, 0), (spot_d, 1)):
+            piece(plane * PLANE + where, part, wx_sem, nbr_x).wait_recv()
+
+    causal = lower_mask(length)
+
+    def score_step(h, carry):
+        c = head_cols(h)
+        kept = jnp.where(causal, contract_cols(q_ref[:, c], k_ref[:, c]), 0.0).astype(jnp.bfloat16)
+        weights[h] = kept
+        normed[h] = contract_mid(kept, v_ref[:, c])
+        return carry
+
+    def norm_step(h, carry):
+        c = head_cols(h)
+        numerator = normed[h] + contract_mid(q_ref[:, c], prefix[h])
+        inv = 1.0 / jnp.sqrt(jnp.mean(numerator * numerator, axis=-1, keepdims=True) + 1e-06)
+        value = numerator * inv
+        normed[h] = value
+        inv_spread[h] = jnp.broadcast_to(inv, (length, HEAD_DIM))
+        attended[:, c] = value.astype(jnp.bfloat16)
+        return carry
+
+    tile = cols
+    n_tiles = rows // tile
+
+    def grad_cols(block):
+        return g_all[block // per_core, :, pl.ds(pl.multiple_of(lax.rem(block, per_core) * cols, cols), cols)]
+
+    def direction_step(k):
+        base = order[k] * PLANE
+
+        def one(n, carry):
+            span = pl.ds(pl.multiple_of(n * tile, tile), tile)
+            total = contract_cols(grad_cols(base), w_all[base, span])
+            for s in range(1, PLANE):
+                total = total + contract_cols(grad_cols(base + s), w_all[base + s, span])
+            if k > 0:
+                total = total + out_dir[:, span]
+            out_dir[:, span] = total
+            return carry
+
+        lax.fori_loop(0, n_tiles, one, 0)
+
+    def p_copy(slot):
+        return pltpu.make_async_remote_copy(
+            src_ref=p_send.at[slot], dst_ref=p_recv.at[slot],
+            send_sem=p_send_sem.at[slot], recv_sem=p_recv_sem.at[slot],
+            device_id=(me, other), device_id_type=MESH,
+        )
+
+    def partial_step(k):
+        def one(s, carry):
+            block = order[k] * PLANE + s
+            term = contract_mid(attended[...], w_all[block]).astype(jnp.bfloat16)
+            slot = lax.rem(block, per_core)
+
+            @pl.when(block // per_core == core)
+            def _():
+                p_own[slot] = term
+
+            @pl.when(block // per_core != core)
+            def _():
+                p_send[slot] = term
+                p_copy(slot).start()
+
+            return carry
+
+        lax.fori_loop(0, PLANE, one, 0)
+
+    lax.fori_loop(0, heads, score_step, 0)
+    arrived(st_send, st_recv, 0)
+
+    def before_step(b, total):
+        low = total.astype(jnp.bfloat16)
+        pre_send[b] = low
+
+        @pl.when(b == me)
+        def _():
+            prefix[me] = low
+
+        return total + st_recv[b].astype(jnp.float32)
+
+    lax.fori_loop(0, blocks, before_step, jnp.zeros((HEAD_DIM, HEAD_DIM), jnp.float32))
+    exchange(pre_send, prefix, 1, True)
+
+    for k in range(1, planes + 1):
+        if k < planes:
+            column_step(k)
+        relay_step(k - 1)
+        if k == 1:
+            own_w.wait()
+            own_g.wait()
+            g_copy.wait()
+        if k == 2:
+            arrived(pre_send, prefix, 1)
+            lax.fori_loop(0, heads, norm_step, 0)
+        if k >= 2:
+            settle(k - 2)
+            direction_step(k - 2)
+            partial_step(k - 2)
+    settle(planes - 1)
+    direction_step(planes - 1)
+
+    def numer_step(h, carry):
+        c = head_cols(h)
+        toward, unit = out_dir[:, c], normed[h]
+        along = jnp.mean(toward * unit, axis=-1, keepdims=True)
+        low = ((toward - unit * along) * inv_spread[h]).astype(jnp.bfloat16)
+        ng[:, c] = low
+        lg_send[h] = contract_rows(q_ref[:, c], low).astype(jnp.bfloat16)
+        return carry
+
+    lax.fori_loop(0, heads, numer_step, 0)
+    lg_recv[me] = lg_send[me]
+    exchange(lg_send, lg_recv, 2, True)
+    partial_step(planes - 1)
+    arrived(lg_send, lg_recv, 2)
+
+    def after_step(i, total):
+        b = blocks - 1 - i
+        low = total.astype(jnp.bfloat16)
+        suf_send[b] = low
+
+        @pl.when(b == me)
+        def _():
+            suffix[me] = low
+
+        return total + lg_recv[b].astype(jnp.float32)
+
+    lax.fori_loop(0, blocks, after_step, jnp.zeros((HEAD_DIM, HEAD_DIM), jnp.float32))
+    exchange(suf_send, suffix, 3, True)
+
+    def pair_step(h, carry):
+        c = head_cols(h)
+        low = ng[:, c]
+        pair = jnp.where(causal, contract_cols(low, v_ref[:, c]), 0.0).astype(jnp.bfloat16)
+        dq_ref[:, c] = (contract_mid(pair, k_ref[:, c]) + contract_cols(low, prefix[h])).astype(jnp.bfloat16)
+        k_part[h] = contract_rows(pair, q_ref[:, c])
+        v_part[h] = contract_rows(weights[h], low)
+        return carry
+
+    lax.fori_loop(0, heads, pair_step, 0)
+
+    def mix_step(slot, carry):
+        p_copy(slot).wait()
+        c = pl.ds(pl.multiple_of(slot * cols, cols), cols)
+        mixed_ref[:, c] = (p_own[slot].astype(jnp.float32) + p_recv[slot].astype(jnp.float32)).astype(jnp.bfloat16)
+        return carry
+
+    lax.fori_loop(0, per_core, mix_step, 0)
+    arrived(suf_send, suffix, 3)
+
+    def last_step(h, carry):
+        c = head_cols(h)
+        dk_ref[:, c] = (k_part[h] + contract_cols(v_ref[:, c], suffix[h])).astype(jnp.bfloat16)
+        dv_ref[:, c] = (v_part[h] + contract_mid(k_ref[:, c], suffix[h])).astype(jnp.bfloat16)
+        return carry
+
+    lax.fori_loop(0, heads, last_step, 0)
+
+    for part in range(2):
+        piece(me, part, wx_sem, nbr_x, True).wait_send()
+        piece(me, part, wy_sem, nbr_y, True).wait_send()
+
+        @pl.when(up_ok)
+        def _():
+            piece(me, part, wz_sem.at[0], up, True).wait_send()
+
+        @pl.when(down_ok)
+        def _():
+            piece(me, part, wz_sem.at[1], down, True).wait_send()
+
+    for k in range(planes):
+        if k:
+            column_step(k, True)
+        relay_step(k, True)
+    exchange(st_send, st_recv, 0, False)
+    exchange(pre_send, prefix, 1, False)
+    exchange(lg_send, lg_recv, 2, False)
+    exchange(suf_send, suffix, 3, False)
+
+
+def fused(blocks, queries, key_rows, values, out_weight, out_grad):
+    length, width = queries.shape
+    heads = width // HEAD_DIM
+    rows, cols = out_weight.shape
+    per_core = blocks // 2
+    low, wide = jnp.bfloat16, jnp.float32
+    state = pltpu.VMEM((blocks, HEAD_DIM, HEAD_DIM), low)
+    by_head = pltpu.VMEM((heads, length, HEAD_DIM), wide)
+    flat = pltpu.VMEM((length, width), low)
+    parts = pltpu.VMEM((per_core, length, cols), low)
+    dma = pltpu.SemaphoreType.DMA
+    out = jax.ShapeDtypeStruct((length, width), low)
+    vmem, anywhere = pl.BlockSpec(memory_space=pltpu.VMEM), pl.BlockSpec(memory_space=pl.ANY)
+    return pl.pallas_call(
+        functools.partial(kernel, blocks),
+        out_shape=(out, out, out, out),
+        in_specs=[vmem, vmem, vmem, anywhere, anywhere],
+        out_specs=(vmem, vmem, vmem, vmem),
+        scratch_shapes=[
+            pltpu.VMEM((blocks, rows, cols), low),
+            pltpu.VMEM((2, length, width), low),
+            state, state, state, state, state, state, state, state,
+            pltpu.VMEM((length, rows), wide),
+            by_head, by_head,
+            pltpu.VMEM((heads, length, length), low),
+            flat, parts, parts, parts, flat, by_head, by_head,
+            dma((blocks, 2)), dma((blocks, 2)), dma((blocks, 2)), dma((2, blocks, 2)),
+            dma((2,)), dma((2,)), dma((4, blocks)), dma((4, blocks)), dma((per_core,)), dma((per_core,)),
+        ],
+        compiler_params=pltpu.CompilerParams(
+            collective_id=0, has_side_effects=True, vmem_limit_bytes=60 * 2**20
+        ),
+    )(queries, key_rows, values, out_weight, out_grad)
+
+
 def solution(mesh):
+    blocks, cores = mesh.shape["seq"], mesh.shape["head"]
+
+    def step(queries, key_rows, values, out_weight, out_grad):
+        heads = queries.shape[1] // HEAD_DIM
+        fits = cores == 2 and blocks % PLANE == 0 and heads == blocks and out_weight.shape[1] % 128 == 0
+        fits = fits and out_weight.shape[0] == queries.shape[1] and out_weight.shape[0] % out_weight.shape[1] == 0
+        if fits and out_weight.shape[1] * blocks == queries.shape[1] * cores:
+            return fused(blocks, queries, key_rows, values, out_weight, out_grad)
+        return per_device(queries, key_rows, values, out_weight, out_grad)
+
     placed = (
         P("seq", "head"),
         P("seq", "head"),
@@ -118,7 +533,7 @@
         P("seq", "head"),
     )
     return jax.shard_map(
-        per_device,
+        step,
         mesh=mesh,
         in_specs=placed,
         out_specs=(P("seq", "head"), P("seq", "head"), P("seq", "head"), P("seq", "head")),

time: 628 us -> 205 us (0.33)
  waiting for transfers between devices: 493 us -> 0 us
  Pallas kernels: 0 us -> 197 us
  other arithmetic: 53.5 us -> 0 us
  matrix products: 49.6 us -> 0 us
  between operations: 14 us -> 0.65 us
  local copies, waits for them, and re-layouts: 15.6 us -> 6.57 us
    all_gather x4 -> x0, waiting for transfers between devices: 491 us -> none  [the longest x1 219 us: per_device(): full_weight = lax.all_gather(out_weight, 'seq', axis=1, tiled=True)]
    pallas_call x0 -> x1, Pallas kernels: none -> 197 us  [fused(): pl.pallas_call(functools.partial(kernel, blocks), out_shape=(out, out, ou...]
    select_n x32 -> x0, other arithmetic: 52 us -> none  [hop(): return jnp.where(reached, new, before)]
    dot_general x14 -> x0, matrix products: 49.6 us -> none  [the longest x1 12.5 us: contract_cols(): lax.dot_general(left_side, right_side, (((1,), (1,)), ((), ())), preferre...]
    unnamed x32 -> x10, local copies, waits for them, and re-layouts: 13 us -> 6.57 us
  transfers between devices with their start and end apart: 5 -> 0, of which waited for: 3 -> 0; matrix products, arithmetic and copies ran while one was open for 15% -> 0% of each run, Pallas kernels for 0% -> 0%
where the time goes in v1:
time: 205 us; the launch traced here: 204 us
  Pallas kernels  197 us (96%)
  local copies, waits for them, and re-layouts  6.57 us (3%)
    pallas_call x1, Pallas kernels, fused(): pl.pallas_call(functools.partial(kernel, blocks), out_shape=(out, out, ou...  197 us
    unnamed x10, local copies, waits for them, and re-layouts  6.57 us

profile of v1, /device:TPU:0, one launch (start us, length us, event | category | flops | bytes accessed | tf_op | source)
XLA Modules:
  0.0 204.4 jit_solution(18424183279245006290)
XLA Ops:
  0.6 197.2 %shard_map.84 = (bf16[256,2048]{1,0:T(8,128)(2,1)}, bf16[256,2048]{1,0:T(8,128)(2,1)}, bf16[256,2048]{1,0:T(8,128)(2,1)}, bf16[256,2048]{1,0:T(8,128)(2,1)}) custom-call(bf16[256,2048]{1,0:T(8,128)(2,1)} %q_ref.1, bf16[256,2048]{1,0:T(8,128)(2,1)} %k_ref.1, bf16[256,2048]{1,0:T(8,128)(2,1)} %v_ref.1, bf16[2048,256]{1,0:T(8,128)(2,1)} %w_ref.1, ...), custom_call_target="tpu_custom_call" | custom-call | tf_op jit(solution)/shard_map/pallas_call | solution.py:495
  197.9 0.0 copy-start.2
  197.9 2.4 %copy.13 = bf16[256,2048]{1,0:T(8,128)(2,1)} copy(bf16[256,2048]{1,0:T(8,128)(2,1)} %get-tuple-element.8) | data formatting | bytes 2097152
  200.3 0.0 copy-done.2
  200.3 0.0 copy-start.1
  200.3 1.0 copy.14
  201.2 0.6 copy-done.1
  201.9 0.0 copy-start
  201.9 1.0 copy.15
  202.8 0.6 copy-done
  203.5 1.0 copy.16
Async XLA Ops:
  197.9 2.4 %copy-start.2 = (bf16[256,2048]{1,0:T(8,128)(2,1)S(1)}, bf16[256,2048]{1,0:T(8,128)(2,1)}, u32[]{:S(2)}) copy-start(bf16[256,2048]{1,0:T(8,128)(2,1)} %get-tuple-element.9) | copy-start | bytes 3145732
  200.3 1.6 copy-start.1
  201.9 1.6 copy-start

commit v2 on v1

--- a/solution.py
+++ b/solution.py
@@ -126,10 +126,9 @@
 
 
 def visit_tables(planes):
-    rows = []
+    half, rows = planes // 2, []
     for own in range(planes):
-        near_low = own < planes - 1 - own
-        rows.append(sorted(range(planes), key=lambda other: (abs(other - own), (other > own) == near_low)))
+        rows.append(sorted(range(planes), key=lambda other: (other // half != own // half, abs(other - own))))
     return rows
 
 
@@ -151,6 +150,7 @@
     core = lax.axis_index("head")
     other = 1 - core
     planes = blocks // PLANE
+    half_planes = planes // 2
     spot = lax.rem(me, PLANE)
     level = me // PLANE
     bit_x, bit_y = lax.rem(spot, 2), spot // 2
@@ -195,6 +195,15 @@
     st_recv[me] = st_send[me]
 
     pl.semaphore_wait(barrier, blocks)
+
+    def leave(src, dst, kind, peer):
+        @pl.when(peer != me)
+        def _():
+            pltpu.make_async_remote_copy(
+                src_ref=src.at[peer], dst_ref=dst.at[me],
+                send_sem=a_send_sem.at[kind, peer], recv_sem=a_recv_sem.at[kind, me],
+                device_id=at_seq(peer), device_id_type=MESH,
+            ).start()
 
     def exchange(src, dst, kind, start):
         def one(i, carry):
@@ -260,15 +269,13 @@
     tables = visit_tables(planes)
     order = [pick([tables[z][k] for z in range(planes)], level) for k in range(planes)]
 
-    def column_step(k, finish=False):
+    def along_z(k, where, finish=False):
         plane = order[k]
-        block = plane * PLANE + spot
+        block = plane * PLANE + where
         going_up = plane < level
         for part in range(2):
             if not finish:
                 piece(block, part, wx_sem, nbr_x).wait_recv()
-                piece(block, part, wx_sem, nbr_x).start()
-                piece(block, part, wy_sem, nbr_y).start()
 
             @pl.when(jnp.logical_and(going_up, up_ok))
             def _():
@@ -280,9 +287,11 @@
                 copy = piece(block, part, wz_sem.at[1], down)
                 copy.wait_send() if finish else copy.start()
 
-            if finish:
-                piece(block, part, wx_sem, nbr_x).wait_send()
-                piece(block, part, wy_sem, nbr_y).wait_send()
+    def across(k, finish=False):
+        block = order[k] * PLANE + spot
+        for part in range(2):
+            for copy in (piece(block, part, wx_sem, nbr_x), piece(block, part, wy_sem, nbr_y)):
+                copy.wait_send() if finish else copy.start()
 
     def relay_step(k, finish=False):
         plane = order[k]
@@ -295,9 +304,25 @@
                 copy.wait_recv()
                 copy.start()
 
+    def cross_step(k, finish=False):
+        block = order[k] * PLANE + spot_d
+        for part in range(2):
+
+            @pl.when(level == half_planes - 1)
+            def _():
+                copy = piece(block, part, wz_sem.at[0], up)
+                copy.wait_send() if finish else copy.start()
+
+            @pl.when(level == half_planes)
+            def _():
+                copy = piece(block, part, wz_sem.at[1], down)
+                copy.wait_send() if finish else copy.start()
+
     def settle(k):
         plane = order[k]
-        for where, part in ((spot_y, 1), (spot_x, 0), (spot_d, 0), (spot_d, 1)):
+        near = ((spot_y, 1), (spot_x, 0), (spot_d, 0), (spot_d, 1))
+        far = ((spot_y, 0), (spot_x, 0), (spot_y, 1), (spot_x, 1))
+        for where, part in near if k < half_planes else far:
             piece(plane * PLANE + where, part, wx_sem, nbr_x).wait_recv()
 
     causal = lower_mask(length)
@@ -367,6 +392,10 @@
         lax.fori_loop(0, PLANE, one, 0)
 
     lax.fori_loop(0, heads, score_step, 0)
+    relay_step(0)
+    along_z(1, spot)
+    across(1)
+    along_z(2, spot)
     arrived(st_send, st_recv, 0)
 
     def before_step(b, total):
@@ -382,23 +411,30 @@
     lax.fori_loop(0, blocks, before_step, jnp.zeros((HEAD_DIM, HEAD_DIM), jnp.float32))
     exchange(pre_send, prefix, 1, True)
 
-    for k in range(1, planes + 1):
-        if k < planes:
-            column_step(k)
-        relay_step(k - 1)
-        if k == 1:
-            own_w.wait()
-            own_g.wait()
-            g_copy.wait()
-        if k == 2:
-            arrived(pre_send, prefix, 1)
-            lax.fori_loop(0, heads, norm_step, 0)
-        if k >= 2:
-            settle(k - 2)
-            direction_step(k - 2)
-            partial_step(k - 2)
-    settle(planes - 1)
-    direction_step(planes - 1)
+    settle(0)
+    cross_step(0)
+    relay_step(1)
+    along_z(3, spot)
+    across(2)
+    own_w.wait()
+    own_g.wait()
+    g_copy.wait()
+    direction_step(0)
+    along_z(2, spot_d)
+    settle(1)
+    cross_step(1)
+    across(3)
+    direction_step(1)
+    arrived(pre_send, prefix, 1)
+    lax.fori_loop(0, heads, norm_step, 0)
+    partial_step(0)
+    along_z(3, spot_d)
+    partial_step(1)
+    settle(2)
+    direction_step(2)
+    partial_step(2)
+    settle(3)
+    direction_step(3)
 
     def numer_step(h, carry):
         c = head_cols(h)
@@ -407,11 +443,16 @@
         low = ((toward - unit * along) * inv_spread[h]).astype(jnp.bfloat16)
         ng[:, c] = low
         lg_send[h] = contract_rows(q_ref[:, c], low).astype(jnp.bfloat16)
+
+        @pl.when(h > 0)
+        def _():
+            leave(lg_send, lg_recv, 2, h - 1)
+
         return carry
 
     lax.fori_loop(0, heads, numer_step, 0)
+    leave(lg_send, lg_recv, 2, heads - 1)
     lg_recv[me] = lg_send[me]
-    exchange(lg_send, lg_recv, 2, True)
     partial_step(planes - 1)
     arrived(lg_send, lg_recv, 2)
 
@@ -469,10 +510,14 @@
         def _():
             piece(me, part, wz_sem.at[1], down, True).wait_send()
 
-    for k in range(planes):
-        if k:
-            column_step(k, True)
+    for k in range(1, planes):
+        along_z(k, spot, True)
+        across(k, True)
+    for k in range(half_planes):
         relay_step(k, True)
+        cross_step(k, True)
+    for k in range(half_planes, planes):
+        along_z(k, spot_d, True)
     exchange(st_send, st_recv, 0, False)
     exchange(pre_send, prefix, 1, False)
     exchange(lg_send, lg_recv, 2, False)
@@ -519,7 +564,7 @@
 
     def step(queries, key_rows, values, out_weight, out_grad):
         heads = queries.shape[1] // HEAD_DIM
-        fits = cores == 2 and blocks % PLANE == 0 and heads == blocks and out_weight.shape[1] % 128 == 0
+        fits = cores == 2 and blocks == PLANE * PLANE and heads == blocks and out_weight.shape[1] % HEAD_DIM == 0
         fits = fits and out_weight.shape[0] == queries.shape[1] and out_weight.shape[0] % out_weight.shape[1] == 0
         if fits and out_weight.shape[1] * blocks == queries.shape[1] * cores:
             return fused(blocks, queries, key_rows, values, out_weight, out_grad)

time: 205 us -> 194 us (0.946)
  Pallas kernels: 197 us -> 186 us
    pallas_call x1, Pallas kernels: 197 us -> 186 us  [fused(): pl.pallas_call(functools.partial(kernel, blocks), out_shape=(out, out, ou...]
where the time goes in v2:
time: 194 us; the launch traced here: 193 us
  Pallas kernels  186 us (96%)
  local copies, waits for them, and re-layouts  6.57 us (3%)
    pallas_call x1, Pallas kernels, fused(): pl.pallas_call(functools.partial(kernel, blocks), out_shape=(out, out, ou...  186 us
    unnamed x10, local copies, waits for them, and re-layouts  6.57 us

profile of v2, /device:TPU:0, one launch (start us, length us, event | category | flops | bytes accessed | tf_op | source)
XLA Modules:
  0.0 193.4 jit_solution(6766562585131550397)
XLA Ops:
  0.6 186.2 %shard_map.84 = (bf16[256,2048]{1,0:T(8,128)(2,1)}, bf16[256,2048]{1,0:T(8,128)(2,1)}, bf16[256,2048]{1,0:T(8,128)(2,1)}, bf16[256,2048]{1,0:T(8,128)(2,1)}) custom-call(bf16[256,2048]{1,0:T(8,128)(2,1)} %q_ref.1, bf16[256,2048]{1,0:T(8,128)(2,1)} %k_ref.1, bf16[256,2048]{1,0:T(8,128)(2,1)} %v_ref.1, bf16[2048,256]{1,0:T(8,128)(2,1)} %w_ref.1, ...), custom_call_target="tpu_custom_call" | custom-call | tf_op jit(solution)/shard_map/pallas_call | solution.py:540
  186.8 0.0 copy-start.2
  186.8 2.4 %copy.13 = bf16[256,2048]{1,0:T(8,128)(2,1)} copy(bf16[256,2048]{1,0:T(8,128)(2,1)} %get-tuple-element.8) | data formatting | bytes 2097152
  189.2 0.0 copy-done.2
  189.2 0.0 copy-start.1
  189.2 1.0 copy.14
  190.2 0.6 copy-done.1
  190.8 0.0 copy-start
  190.8 1.0 copy.15
  191.8 0.6 copy-done
  192.4 1.0 copy.16
Async XLA Ops:
  186.8 2.4 %copy-start.2 = (bf16[256,2048]{1,0:T(8,128)(2,1)S(1)}, bf16[256,2048]{1,0:T(8,128)(2,1)}, u32[]{:S(2)}) copy-start(bf16[256,2048]{1,0:T(8,128)(2,1)} %get-tuple-element.9) | copy-start | bytes 3145732
  189.2 1.6 copy-start.1
  190.8 1.6 copy-start

commit v3 on v2

--- a/solution.py
+++ b/solution.py
@@ -140,9 +140,9 @@
 
 
 def kernel(
-    blocks, q_ref, k_ref, v_ref, w_ref, g_ref,
+    blocks, q_in, k_in, v_in, w_ref, g_ref,
     mixed_ref, dq_ref, dk_ref, dv_ref,
-    w_all, g_all, st_send, st_recv, pre_send, prefix, lg_send, lg_recv, suf_send, suffix,
+    q_ref, k_ref, v_ref, w_all, g_all, st_send, st_recv, pre_send, prefix, lg_send, lg_recv, suf_send, suffix,
     out_dir, normed, inv_spread, weights, attended, p_own, p_send, p_recv, ng, k_part, v_part,
     w_recv_sem, wx_sem, wy_sem, wz_sem, local_sem, g_sem, a_send_sem, a_recv_sem, p_send_sem, p_recv_sem,
 ):
@@ -169,6 +169,11 @@
     nbr_x = level * PLANE + spot_x
     nbr_y = level * PLANE + spot_y
 
+    q_load = pltpu.make_async_copy(q_in, q_ref, local_sem.at[2])
+    k_load = pltpu.make_async_copy(k_in, k_ref, local_sem.at[3])
+    v_load = pltpu.make_async_copy(v_in, v_ref, local_sem.at[4])
+    k_load.start()
+    v_load.start()
     barrier = pltpu.get_barrier_semaphore()
 
     def greet(i, carry):
@@ -180,8 +185,11 @@
 
     own_w = pltpu.make_async_copy(w_ref, w_all.at[me], local_sem.at[0])
     own_g = pltpu.make_async_copy(g_ref, g_all.at[core], local_sem.at[1])
+    q_load.start()
     own_w.start()
     own_g.start()
+    k_load.wait()
+    v_load.wait()
 
     def head_cols(h):
         return pl.ds(pl.multiple_of(h * HEAD_DIM, HEAD_DIM), HEAD_DIM)
@@ -269,27 +277,35 @@
     tables = visit_tables(planes)
     order = [pick([tables[z][k] for z in range(planes)], level) for k in range(planes)]
 
+    def passing(k):
+        return jnp.where(order[k] < level, up_ok, down_ok)
+
     def along_z(k, where, finish=False):
         plane = order[k]
         block = plane * PLANE + where
         going_up = plane < level
         for part in range(2):
-            if not finish:
-                piece(block, part, wx_sem, nbr_x).wait_recv()
-
-            @pl.when(jnp.logical_and(going_up, up_ok))
-            def _():
-                copy = piece(block, part, wz_sem.at[0], up)
-                copy.wait_send() if finish else copy.start()
-
-            @pl.when(jnp.logical_and(jnp.logical_not(going_up), down_ok))
-            def _():
-                copy = piece(block, part, wz_sem.at[1], down)
-                copy.wait_send() if finish else copy.start()
+            for sems, way, go in ((wz_sem.at[0], up, going_up), (wz_sem.at[1], down, jnp.logical_not(going_up))):
+
+                @pl.when(jnp.logical_and(go, passing(k)))
+                def _():
+                    copy = piece(block, part, sems, way)
+                    if finish:
+                        copy.wait_send()
+                    else:
+                        copy.wait_recv()
+                        copy.start()
+
+    def end_of_z(k, where, part):
+        @pl.when(jnp.logical_not(passing(k)))
+        def _():
+            piece(order[k] * PLANE + where, part, wx_sem, nbr_x).wait_recv()
 
     def across(k, finish=False):
         block = order[k] * PLANE + spot
         for part in range(2):
+            if not finish:
+                end_of_z(k, spot, part)
             for copy in (piece(block, part, wx_sem, nbr_x), piece(block, part, wy_sem, nbr_y)):
                 copy.wait_send() if finish else copy.start()
 
@@ -324,6 +340,9 @@
         far = ((spot_y, 0), (spot_x, 0), (spot_y, 1), (spot_x, 1))
         for where, part in near if k < half_planes else far:
             piece(plane * PLANE + where, part, wx_sem, nbr_x).wait_recv()
+        if k >= half_planes:
+            for part in range(2):
+                end_of_z(k, spot_d, part)
 
     causal = lower_mask(length)
 
@@ -391,6 +410,7 @@
 
         lax.fori_loop(0, PLANE, one, 0)
 
+    q_load.wait()
     lax.fori_loop(0, heads, score_step, 0)
     relay_step(0)
     along_z(1, spot)
@@ -413,8 +433,8 @@
 
     settle(0)
     cross_step(0)
+    along_z(3, spot)
     relay_step(1)
-    along_z(3, spot)
     across(2)
     own_w.wait()
     own_g.wait()
@@ -524,6 +544,27 @@
     exchange(suf_send, suffix, 3, False)
 
 
+def store_kernel(*refs):
+    count = (len(refs) - 1) // 2
+    copies = [pltpu.make_async_copy(refs[i], refs[count + i], refs[-1].at[i]) for i in range(count)]
+    for copy in copies:
+        copy.start()
+    for copy in copies:
+        copy.wait()
+
+
+def store(*arrays):
+    count = len(arrays)
+    return pl.pallas_call(
+        store_kernel,
+        out_shape=tuple(jax.ShapeDtypeStruct(a.shape, a.dtype) for a in arrays),
+        in_specs=[pl.BlockSpec(memory_space=pltpu.VMEM)] * count,
+        out_specs=(pl.BlockSpec(memory_space=pltpu.HBM),) * count,
+        scratch_shapes=[pltpu.SemaphoreType.DMA((count,))],
+        compiler_params=pltpu.CompilerParams(vmem_limit_bytes=8 * 2**20),
+    )(*arrays)
+
+
 def fused(blocks, queries, key_rows, values, out_weight, out_grad):
     length, width = queries.shape
     heads = width // HEAD_DIM
@@ -536,13 +577,14 @@
     parts = pltpu.VMEM((per_core, length, cols), low)
     dma = pltpu.SemaphoreType.DMA
     out = jax.ShapeDtypeStruct((length, width), low)
-    vmem, anywhere = pl.BlockSpec(memory_space=pltpu.VMEM), pl.BlockSpec(memory_space=pl.ANY)
-    return pl.pallas_call(
+    vmem, in_hbm = pl.BlockSpec(memory_space=pltpu.VMEM), pl.BlockSpec(memory_space=pltpu.HBM)
+    results = pl.pallas_call(
         functools.partial(kernel, blocks),
         out_shape=(out, out, out, out),
-        in_specs=[vmem, vmem, vmem, anywhere, anywhere],
+        in_specs=[in_hbm] * 5,
         out_specs=(vmem, vmem, vmem, vmem),
         scratch_shapes=[
+            flat, flat, flat,
             pltpu.VMEM((blocks, rows, cols), low),
             pltpu.VMEM((2, length, width), low),
             state, state, state, state, state, state, state, state,
@@ -551,12 +593,13 @@
             pltpu.VMEM((heads, length, length), low),
             flat, parts, parts, parts, flat, by_head, by_head,
             dma((blocks, 2)), dma((blocks, 2)), dma((blocks, 2)), dma((2, blocks, 2)),
-            dma((2,)), dma((2,)), dma((4, blocks)), dma((4, blocks)), dma((per_core,)), dma((per_core,)),
+            dma((5,)), dma((2,)), dma((4, blocks)), dma((4, blocks)), dma((per_core,)), dma((per_core,)),
         ],
         compiler_params=pltpu.CompilerParams(
-            collective_id=0, has_side_effects=True, vmem_limit_bytes=60 * 2**20
+            collective_id=0, has_side_effects=True, vmem_limit_bytes=46 * 2**20
         ),
     )(queries, key_rows, values, out_weight, out_grad)
+    return store(*results)
 
 
 def solution(mesh):

time: 194 us -> 177 us (0.912)
  Pallas kernels: 186 us -> 173 us
  local copies, waits for them, and re-layouts: 6.57 us -> 3.67 us
    pallas_call x1, Pallas kernels: 186 us -> 171 us  [fused(): pl.pallas_call(functools.partial(kernel, blocks), out_shape=(out, out, ou...]
    unnamed x10 -> x6, local copies, waits for them, and re-layouts: 6.57 us -> 3.67 us
    pallas_call x0 -> x1, Pallas kernels: none -> 2.04 us  [store(): pl.pallas_call(store_kernel, out_shape=tuple((jax.ShapeDtypeStruct(a.shap...]
where the time goes in v3:
time: 177 us
  Pallas kernels  173 us (98%)
  local copies, waits for them, and re-layouts  3.67 us (2%)
    pallas_call x1, Pallas kernels, fused(): pl.pallas_call(functools.partial(kernel, blocks), out_shape=(out, out, ou...  171 us
    unnamed x6, local copies, waits for them, and re-layouts  3.67 us

profile of v3, /device:TPU:0, one launch (start us, length us, event | category | flops | bytes accessed | tf_op | source)
XLA Modules:
  0.0 176.9 jit_solution(1620838712507620947)
XLA Ops:
  0.6 0.0 copy-start
  0.6 1.2 copy-done
  1.9 0.0 copy-start.1
  1.9 1.2 copy-done.1
  3.1 0.0 copy-start.2
  3.1 1.2 copy-done.2
  4.3 170.5 %shard_map.84 = (bf16[256,2048]{1,0:T(8,128)(2,1)S(1)}, bf16[256,2048]{1,0:T(8,128)(2,1)S(1)}, bf16[256,2048]{1,0:T(8,128)(2,1)S(1)}, bf16[256,2048]{1,0:T(8,128)(2,1)S(1)}) custom-call(bf16[256,2048]{1,0:T(8,128)(2,1)S(1)} %copy-done, bf16[256,2048]{1,0:T(8,128)(2,1)S(1)} %copy-done.1, bf16[256,2048]{1,0:T(8,128)(2,1)S(1)} %copy-done.2, ...), custom_call_target="tpu_custom_call" | custom-call | tf_op jit(solution)/shard_map/pallas_call | solution.py:581
  174.8 2.0 %shard_map.85 = (bf16[256,2048]{1,0:T(8,128)(2,1)}, bf16[256,2048]{1,0:T(8,128)(2,1)}, bf16[256,2048]{1,0:T(8,128)(2,1)}, bf16[256,2048]{1,0:T(8,128)(2,1)}) custom-call(bf16[256,2048]{1,0:T(8,128)(2,1)S(1)} %get-tuple-element.8.refs_0_, bf16[256,2048]{1,0:T(8,128)(2,1)S(1)} %get-tuple-element.9.refs_1_, bf16[256,2048]{1,0:T(8,128)(2,1)S(1)} %get-tuple-element.10.refs_2_, ...), custom_call_target="tpu_custom_call" | custom-call | tf_op jit(solution)/shard_map/pallas_call | solution.py:558
Async XLA Ops:
  0.6 1.2 copy-start
  1.9 1.2 copy-start.1
  3.1 1.2 copy-start.2

commit v4 on v3

--- a/solution.py
+++ b/solution.py
@@ -144,13 +144,18 @@
     mixed_ref, dq_ref, dk_ref, dv_ref,
     q_ref, k_ref, v_ref, w_all, g_all, st_send, st_recv, pre_send, prefix, lg_send, lg_recv, suf_send, suffix,
     out_dir, normed, inv_spread, weights, attended, p_own, p_send, p_recv, ng, k_part, v_part,
+    x_send, x_recv,
     w_recv_sem, wx_sem, wy_sem, wz_sem, local_sem, g_sem, a_send_sem, a_recv_sem, p_send_sem, p_recv_sem,
+    x_send_sem, x_recv_sem,
 ):
     me = lax.axis_index("seq")
     core = lax.axis_index("head")
     other = 1 - core
     planes = blocks // PLANE
     half_planes = planes // 2
+    size = blocks // 2
+    share = st_send.shape[0] // size
+    team, rank = me // size, lax.rem(me, size)
     spot = lax.rem(me, PLANE)
     level = me // PLANE
     bit_x, bit_y = lax.rem(spot, 2), spot // 2
@@ -200,53 +205,82 @@
         return carry
 
     lax.fori_loop(0, heads, make_state, 0)
-    st_recv[me] = st_send[me]
+    st_recv[rank] = st_send[pl.ds(rank * share, share)]
 
     pl.semaphore_wait(barrier, blocks)
 
+    def state_copy(src, dst, kind, peer):
+        return pltpu.make_async_remote_copy(
+            src_ref=src(peer), dst_ref=dst(rank),
+            send_sem=a_send_sem.at[kind, peer], recv_sem=a_recv_sem.at[kind, rank],
+            device_id=at_seq(team * size + peer), device_id_type=MESH,
+        )
+
     def leave(src, dst, kind, peer):
-        @pl.when(peer != me)
-        def _():
-            pltpu.make_async_remote_copy(
-                src_ref=src.at[peer], dst_ref=dst.at[me],
-                send_sem=a_send_sem.at[kind, peer], recv_sem=a_recv_sem.at[kind, me],
-                device_id=at_seq(peer), device_id_type=MESH,
-            ).start()
+        @pl.when(peer != rank)
+        def _():
+            state_copy(src, dst, kind, peer).start()
 
     def exchange(src, dst, kind, start):
         def one(i, carry):
-            peer = lax.rem(me + i, blocks)
-            copy = pltpu.make_async_remote_copy(
-                src_ref=src.at[peer], dst_ref=dst.at[me],
-                send_sem=a_send_sem.at[kind, peer], recv_sem=a_recv_sem.at[kind, me],
-                device_id=at_seq(peer), device_id_type=MESH,
-            )
-            if start:
-                copy.start()
-            else:
-                copy.wait_send()
+            copy = state_copy(src, dst, kind, lax.rem(rank + i, size))
+            copy.start() if start else copy.wait_send()
             return carry
 
-        lax.fori_loop(1, blocks, one, 0)
+        lax.fori_loop(1, size, one, 0)
 
     def arrived(src, dst, kind):
         def one(i, carry):
-            peer = lax.rem(me + i, blocks)
+            peer = lax.rem(rank + i, size)
             pltpu.make_async_remote_copy(
-                src_ref=src.at[me], dst_ref=dst.at[peer],
-                send_sem=a_send_sem.at[kind, me], recv_sem=a_recv_sem.at[kind, peer],
-                device_id=at_seq(peer), device_id_type=MESH,
+                src_ref=src(rank), dst_ref=dst(peer),
+                send_sem=a_send_sem.at[kind, rank], recv_sem=a_recv_sem.at[kind, peer],
+                device_id=at_seq(team * size + peer), device_id_type=MESH,
             ).wait_recv()
             return carry
 
-        lax.fori_loop(1, blocks, one, 0)
+        lax.fori_loop(1, size, one, 0)
+
+    def pair_of(ref):
+        return lambda owner: ref.at[pl.ds(owner * share, share)]
+
+    def slot_of(ref):
+        return lambda owner: ref.at[owner]
+
+    def team_total(kind):
+        return pltpu.make_async_remote_copy(
+            src_ref=x_send.at[kind], dst_ref=x_recv.at[kind],
+            send_sem=x_send_sem.at[kind], recv_sem=x_recv_sem.at[kind],
+            device_id=at_seq((1 - team) * size + rank), device_id_type=MESH,
+        )
+
+    def running(first_team, kind, source, low_send, low_own, backwards):
+        @pl.when(team == first_team)
+        def _():
+            x_recv[kind] = jnp.zeros(x_recv.shape[1:], jnp.float32)
+
+        @pl.when(team != first_team)
+        def _():
+            team_total(kind).wait_recv()
+
+        def one(i, total):
+            at = size - 1 - i if backwards else i
+            low_send[at] = total.astype(jnp.bfloat16)
+            return total + source[at].astype(jnp.float32)
+
+        x_send[kind] = lax.fori_loop(0, size, one, x_recv[kind])
+        low_own[pl.ds(rank * share, share)] = low_send[rank]
+
+        @pl.when(team == first_team)
+        def _():
+            team_total(kind).start()
 
     g_copy = pltpu.make_async_remote_copy(
         src_ref=g_ref, dst_ref=g_all.at[core], send_sem=g_sem.at[0], recv_sem=g_sem.at[1],
         device_id=(me, other), device_id_type=MESH,
     )
     g_copy.start()
-    exchange(st_send, st_recv, 0, True)
+    exchange(pair_of(st_send), slot_of(st_recv), 0, True)
 
     def piece(block, part, sems, target, own=False):
         span = pl.ds(part * half, half)
@@ -416,21 +450,9 @@
     along_z(1, spot)
     across(1)
     along_z(2, spot)
-    arrived(st_send, st_recv, 0)
-
-    def before_step(b, total):
-        low = total.astype(jnp.bfloat16)
-        pre_send[b] = low
-
-        @pl.when(b == me)
-        def _():
-            prefix[me] = low
-
-        return total + st_recv[b].astype(jnp.float32)
-
-    lax.fori_loop(0, blocks, before_step, jnp.zeros((HEAD_DIM, HEAD_DIM), jnp.float32))
-    exchange(pre_send, prefix, 1, True)
-
+    arrived(pair_of(st_send), slot_of(st_recv), 0)
+    running(0, 0, st_recv, pre_send, prefix, False)
+    exchange(slot_of(pre_send), pair_of(prefix), 1, True)
     settle(0)
     cross_step(0)
     along_z(3, spot)
@@ -445,7 +467,7 @@
     cross_step(1)
     across(3)
     direction_step(1)
-    arrived(pre_send, prefix, 1)
+    arrived(slot_of(pre_send), pair_of(prefix), 1)
     lax.fori_loop(0, heads, norm_step, 0)
     partial_step(0)
     along_z(3, spot_d)
@@ -464,31 +486,19 @@
         ng[:, c] = low
         lg_send[h] = contract_rows(q_ref[:, c], low).astype(jnp.bfloat16)
 
-        @pl.when(h > 0)
-        def _():
-            leave(lg_send, lg_recv, 2, h - 1)
+        @pl.when(jnp.logical_and(h > 0, lax.rem(h, share) == 0))
+        def _():
+            leave(pair_of(lg_send), slot_of(lg_recv), 2, h // share - 1)
 
         return carry
 
     lax.fori_loop(0, heads, numer_step, 0)
-    leave(lg_send, lg_recv, 2, heads - 1)
-    lg_recv[me] = lg_send[me]
+    leave(pair_of(lg_send), slot_of(lg_recv), 2, size - 1)
+    lg_recv[rank] = lg_send[pl.ds(rank * share, share)]
     partial_step(planes - 1)
-    arrived(lg_send, lg_recv, 2)
-
-    def after_step(i, total):
-        b = blocks - 1 - i
-        low = total.astype(jnp.bfloat16)
-        suf_send[b] = low
-
-        @pl.when(b == me)
-        def _():
-            suffix[me] = low
-
-        return total + lg_recv[b].astype(jnp.float32)
-
-    lax.fori_loop(0, blocks, after_step, jnp.zeros((HEAD_DIM, HEAD_DIM), jnp.float32))
-    exchange(suf_send, suffix, 3, True)
+    arrived(pair_of(lg_send), slot_of(lg_recv), 2)
+    running(1, 1, lg_recv, suf_send, suffix, True)
+    exchange(slot_of(suf_send), pair_of(suffix), 3, True)
 
     def pair_step(h, carry):
         c = head_cols(h)
@@ -508,7 +518,7 @@
         return carry
 
     lax.fori_loop(0, per_core, mix_step, 0)
-    arrived(suf_send, suffix, 3)
+    arrived(slot_of(suf_send), pair_of(suffix), 3)
 
     def last_step(h, carry):
         c = head_cols(h)
@@ -538,10 +548,15 @@
         cross_step(k, True)
     for k in range(half_planes, planes):
         along_z(k, spot_d, True)
-    exchange(st_send, st_recv, 0, False)
-    exchange(pre_send, prefix, 1, False)
-    exchange(lg_send, lg_recv, 2, False)
-    exchange(suf_send, suffix, 3, False)
+    exchange(pair_of(st_send), slot_of(st_recv), 0, False)
+    exchange(slot_of(pre_send), pair_of(prefix), 1, False)
+    exchange(pair_of(lg_send), slot_of(lg_recv), 2, False)
+    exchange(slot_of(suf_send), pair_of(suffix), 3, False)
+    for kind in range(2):
+
+        @pl.when(team == kind)
+        def _():
+            team_total(kind).wait_send()
 
 
 def store_kernel(*refs):
@@ -571,7 +586,11 @@
     rows, cols = out_weight.shape
     per_core = blocks // 2
     low, wide = jnp.bfloat16, jnp.float32
-    state = pltpu.VMEM((blocks, HEAD_DIM, HEAD_DIM), low)
+    size = blocks // 2
+    share = heads // size
+    state = pltpu.VMEM((heads, HEAD_DIM, HEAD_DIM), low)
+    slots = pltpu.VMEM((size, share, HEAD_DIM, HEAD_DIM), low)
+    totals = pltpu.VMEM((2, share, HEAD_DIM, HEAD_DIM), wide)
     by_head = pltpu.VMEM((heads, length, HEAD_DIM), wide)
     flat = pltpu.VMEM((length, width), low)
     parts = pltpu.VMEM((per_core, length, cols), low)
@@ -587,16 +606,18 @@
             flat, flat, flat,
             pltpu.VMEM((blocks, rows, cols), low),
             pltpu.VMEM((2, length, width), low),
-            state, state, state, state, state, state, state, state,
+            state, slots, slots, state, state, slots, slots, state,
             pltpu.VMEM((length, rows), wide),
             by_head, by_head,
             pltpu.VMEM((heads, length, length), low),
             flat, parts, parts, parts, flat, by_head, by_head,
+            totals, totals,
             dma((blocks, 2)), dma((blocks, 2)), dma((blocks, 2)), dma((2, blocks, 2)),
             dma((5,)), dma((2,)), dma((4, blocks)), dma((4, blocks)), dma((per_core,)), dma((per_core,)),
+            dma((2,)), dma((2,)),
         ],
         compiler_params=pltpu.CompilerParams(
-            collective_id=0, has_side_effects=True, vmem_limit_bytes=46 * 2**20
+            collective_id=0, has_side_effects=True, vmem_limit_bytes=49 * 2**20
         ),
     )(queries, key_rows, values, out_weight, out_grad)
     return store(*results)

time: 177 us -> 171 us (0.966)
  Pallas kernels: 173 us -> 169 us
  local copies, waits for them, and re-layouts: 3.67 us -> 0 us
    unnamed x6 -> x0, local copies, waits for them, and re-layouts: 3.67 us -> none
    pallas_call x1, Pallas kernels: 171 us -> 167 us  [fused(): pl.pallas_call(functools.partial(kernel, blocks), out_shape=(out, out, ou...]
where the time goes in v4:
time: 171 us; the launch traced here: 170 us
  Pallas kernels  169 us (99%)
    pallas_call x1, Pallas kernels, fused(): pl.pallas_call(functools.partial(kernel, blocks), out_shape=(out, out, ou...  167 us

profile of v4, /device:TPU:0, one launch (start us, length us, event | category | flops | bytes accessed | tf_op | source)
XLA Modules:
  0.0 169.9 jit_solution(16912747114811568568)
XLA Ops:
  0.6 167.2 %shard_map.84 = (bf16[256,2048]{1,0:T(8,128)(2,1)S(1)}, bf16[256,2048]{1,0:T(8,128)(2,1)S(1)}, bf16[256,2048]{1,0:T(8,128)(2,1)S(1)}, bf16[256,2048]{1,0:T(8,128)(2,1)S(1)}) custom-call(bf16[256,2048]{1,0:T(8,128)(2,1)} %q_in.1, bf16[256,2048]{1,0:T(8,128)(2,1)} %k_in.1, bf16[256,2048]{1,0:T(8,128)(2,1)} %v_in.1, bf16[2048,256]{1,0:T(8,128)(2,1)} %w_ref.1, ...), custom_call_target="tpu_custom_call" | custom-call | tf_op jit(solution)/shard_map/pallas_call | solution.py:600
  167.8 2.0 %shard_map.85 = (bf16[256,2048]{1,0:T(8,128)(2,1)}, bf16[256,2048]{1,0:T(8,128)(2,1)}, bf16[256,2048]{1,0:T(8,128)(2,1)}, bf16[256,2048]{1,0:T(8,128)(2,1)}) custom-call(bf16[256,2048]{1,0:T(8,128)(2,1)S(1)} %get-tuple-element.8.refs_0_, bf16[256,2048]{1,0:T(8,128)(2,1)S(1)} %get-tuple-element.9.refs_1_, bf16[256,2048]{1,0:T(8,128)(2,1)S(1)} %get-tuple-element.10.refs_2_, ...), custom_call_target="tpu_custom_call" | custom-call | tf_op jit(solution)/shard_map/pallas_call | solution.py:573
